TPU v7x, 256 devices: a whole 4x4x8 slice. The times are simulated.
256 devices in a mesh: row: 32 (over y, x, core), col: 8 (over z).
Axes of the slice: x: 4, y: 4, z: 8, core: 2. Of those that a mesh axis runs over, the one named last changes fastest.
Arguments:
- panel: float32 [24576, 256], P('row', 'col'), may hold values from -6 to 6
- trailing: float32 [24576, 12032], P('row', 'col'), may hold values from -6 to 6
Outputs:
- projections: float32 [12032, 256], P('col')
- remainder: float32 [24576, 12032], P('row', 'col')
All inputs are finite; a program needn't handle non-finite values.
Results may differ from a plain program's by a relative error of at most 0.000075.
Values sent between devices are 32-bit elements; how exact they have to be, the bound alone decides.
A program may use at most 64 MiB of HBM per device.

v0:
```python
import jax
import jax.numpy as jnp
from jax import lax
from jax.sharding import PartitionSpec as P


def cross_rows(left, right):
    return lax.dot_general(
        left,
        right,
        (((0,), (0,)), ((), ())),
        precision=lax.Precision.HIGHEST,
        preferred_element_type=jnp.float32,
    )


def solve_right(lower_factor, terms):
    return jax.scipy.linalg.solve_triangular(lower_factor, terms.T, lower=True).T


def per_device(panel, trailing):
    panel_full = lax.all_gather(panel, "col", axis=1, tiled=True)
    panel_gram = lax.psum(cross_rows(panel_full, panel_full), "row")
    lower_factor = jnp.linalg.cholesky(panel_gram)
    orthonormal = solve_right(lower_factor, panel_full)
    cross_terms = lax.psum(cross_rows(trailing, panel_full), "row")
    projections = solve_right(lower_factor, cross_terms)
    update = lax.dot_general(
        orthonormal,
        projections,
        (((1,), (1,)), ((), ())),
        precision=lax.Precision.HIGHEST,
        preferred_element_type=jnp.float32,
    )
    remainder = trailing - update
    return (projections, remainder)


def solution(mesh):
    return jax.shard_map(
        per_device,
        mesh=mesh,
        in_specs=(P("row", "col"), P("row", "col")),
        out_specs=(P("col", None), P("row", "col")),
        check_vma=False,
    )
```

profile of v0, /device:TPU:1, one launch (start us, length us, event | category | flops | bytes accessed | tf_op | source)
XLA Modules:
  0.0 242.3 jit_solution(3756788934562251100)
XLA Ops:
  7.2 0.0 all-reduce.4.cloned.1.call-start
  7.2 24.6 %all_gather.3 = f32[768,256]{0,1:T(8,128)S(1)} all-gather(f32[768,32]{0,1:T(8,128)} %param.2), channel_id=1, replica_groups=mesh['row'=32,'col'=8] {'col'}, dimensions={1}, use_global_device_ids=true | all-gather | bytes 884736 | tf_op jit(solution)/shard_map/all_gather | solution.py:22
  31.8 1.5 fusion.18
  33.4 7.3 %fusion.19 = f32[256,1504]{0,1:T(8,128)} fusion(f32[768,256]{0,1:T(8,128)S(1)} %all_gather.3, f32[768,1504]{0,1:T(8,128)} %param.3), kind=kOutput, calls=%fused_computation.41 | convolution fusion | flops 3548381184 | bytes 6946816 | tf_op jit(solution)/shard_map/dot_general | solution.py:8
  40.7 0.0 all-reduce.4.cloned.1.call-update
  40.7 122.1 %all-reduce.4.cloned.1.call-done = (f32[256,1504]{0,1:T(8,128)}, f32[256,256]{0,1:T(8,128)}) async-done(((f32[256,1504]{0,1:T(8,128)}, f32[256,256]{0,1:T(8,128)}), (f32[256,1504]{0,1:T(8,128)}, f32[256,256]{0,1:T(8,128)})) %all-reduce.4.cloned.1.call-update) | async-done | bytes 1802256 | tf_op jit(solution)/shard_map/psum | solution.py:26
  162.8 1.1 copy.5
  163.9 0.0 slice-start
  163.9 1.0 fusion.8
  164.9 11.7 %cholesky.50 = f32[128,128]{1,0:T(8,128)S(1)} custom-call(f32[128,128]{1,0:T(8,128)S(1)} %cholesky.118), custom_call_target="Cholesky" | custom-call | tf_op jit(solution)/shard_map/jit(cholesky)/cholesky | solution.py:24
  176.7 9.8 %custom-call.18 = f32[1,128,128]{1,2,0:T(8,128)S(1)} custom-call(f32[1,128,128]{2,1,0:T(8,128)S(1)} %get-tuple-element.25), custom_call_target="InvertDiagBlocksLowerTriangular" | custom-call | tf_op jit(solution)/shard_map/jit(cholesky)/cholesky | solution.py:24
  186.5 0.2 constant_dynamic-update-slice_fusion.1
  186.8 0.3 convolution_subtract_fusion.3
  187.0 11.9 %cholesky.105 = f32[128,128]{1,0:T(8,128)S(1)} custom-call(f32[128,128]{1,0:T(8,128)S(1)} %convolution_subtract_fusion.3), custom_call_target="Cholesky" | custom-call | tf_op jit(solution)/shard_map/jit(cholesky)/cholesky | solution.py:24
  198.9 0.6 compare_reduce_fusion
  200.9 0.1 triangular_solve.72
  201.0 4.0 %while.1 = (s32[]{:T(128)}, f32[256,256]{1,0:T(8,128)S(1)}, s32[2,2]{1,0:T(2,128)S(1)}, f32[2,128,128]{2,1,0:T(8,128)S(1)}, s32[]{:T(128)}) while((s32[]{:T(128)}, f32[256,256]{1,0:T(8,128)S(1)}, s32[2,2]{1,0:T(2,128)S(1)}, f32[2,128,128]{2,1,0:T(8,128)S(1)}, s32[]{:T(128)}) %tuple.27), condition=%wide.while_cond, body=%wide.while_body.sunk | while | flops 2 | bytes 131181 | solution.py:18
  201.0 0.6 fusion.31
  201.6 1.4 bitcast_dynamic-update-slice_fusion.2
  203.0 0.6 fusion.31
  203.6 1.4 bitcast_dynamic-update-slice_fusion.2
  205.0 0.0 copy-start
  205.0 19.7 %custom-call.19 = f32[2,128,128]{1,2,0:T(8,128)S(1)} custom-call(f32[2,128,128]{2,1,0:T(8,128)S(1)} %get-tuple-element.9), custom_call_target="InvertDiagBlocksLowerTriangular" | custom-call | tf_op jit(solution)/shard_map/jit(_solve_triangular)/triangular_solve | solution.py:18
  224.7 0.5 fusion.6
  225.2 0.5 convolution_subtract_fusion.2
  225.7 0.5 fusion.12
  226.2 0.0 copy-done
  226.2 0.0 slice-start.1
  226.2 0.8 fusion.4
  227.0 0.8 convolution_subtract_fusion.1
  227.8 0.8 fusion.13
  228.6 1.2 fusion
  229.8 0.0 slice-done
  229.8 0.0 slice-done.1
  229.8 5.6 %convolution_subtract_fusion = f32[768,1504]{0,1:T(8,128)} fusion(f32[768,1504]{0,1:T(8,128)S(1)} %bitcast.45, f32[128,1504]{0,1:T(8,128)S(1)} %fusion.13, f32[128,1504]{0,1:T(8,128)S(1)} %fusion.4, f32[128,768]{1,0:T(8,128)S(1)} %fusion.12, f32[128,768]{1,0:T(8,128)S(1)} %fusion.6), kind=kOutput, calls=%fused_computation.2 | convolution fusion | flops 3550117888 | bytes 11567104 | tf_op jit(solution)/shard_map/dot_general | solution.py:28
  (10 shorter events, 0.1 us)
Async XLA Ops:
  7.2 155.6 %all-reduce.4.cloned.1.call-start = ((), (), s32[]{:S(2)}) async-start(), calls=%async_computation | async-start | bytes 3604480 | tf_op jit(solution)/shard_map/psum | solution.py:26
  163.9 65.9 %slice-start = ((s8[4620288]{0:T(1024)(128)(4,1)}), s8[425984]{0:T(1024)(128)(4,1)S(1)}, s32[]{:S(2)}) async-start(s8[4620288]{0:T(1024)(128)(4,1)} %bitcast.44), calls=%async_computation.1 | async-start | bytes 851968
  205.0 21.2 %copy-start = (f32[256,1504]{0,1:T(8,128)S(1)}, f32[256,1504]{0,1:T(8,128)}, u32[]{:S(2)}) copy-start(f32[256,1504]{0,1:T(8,128)} %get-tuple-element.18) | copy-start | bytes 4620292
  226.2 3.6 %slice-start.1 = ((s8[4620288]{0:T(1024)(128)(4,1)}), s8[4194304]{0:T(1024)(128)(4,1)S(1)}, s32[]{:S(2)}) async-start(s8[4620288]{0:T(1024)(128)(4,1)} %bitcast.44), calls=%async_computation.2 | async-start | bytes 8388608
Sparse Core Ops, SparseCore 0:
  40.8 121.9 all-reduce.3
where the time goes:
time: 243 us; the launch traced here: 242 us
  waiting for transfers between devices  122 us (50%)
  other arithmetic  56.1 us (23%)
  blocking collectives  24.6 us (10%)
  matrix products  18.8 us (8%)
  between operations  15.5 us (6%)
  local copies, waits for them, and re-layouts  5.15 us (2%)
    psum x1, waiting for transfers between devices, per_device(): cross_terms = lax.psum(cross_rows(trailing, panel_full), 'row')  122 us
    another operation x6, other arithmetic, per_device(): lower_factor = jnp.linalg.cholesky(panel_gram)  34.1 us
    all_gather x1, blocking collectives, per_device(): panel_full = lax.all_gather(panel, 'col', axis=1, tiled=True)  24.6 us
    another operation x3, other arithmetic, solve_right(): jax.scipy.linalg.solve_triangular(lower_factor, terms.T, lower=True)  19.7 us
    dot_general x2, matrix products, cross_rows(): lax.dot_general(left, right, (((0,), (0,)), ((), ())), precision=lax.Prec...  8.82 us
    dot_general x1, matrix products, per_device(): lax.dot_general(orthonormal, projections, (((1,), (1,)), ((), ())), preci...  5.64 us
  transfers between devices with their start and end apart: 1, of which 1 were waited for; matrix products, arithmetic and copies ran while one was open for 0% of the time, Pallas kernels for 0%

commit v1 on v0

v1 whole, which is shorter than its diff:
```python
import jax
import jax.numpy as jnp
from jax import lax
from jax.experimental import pallas as pl
from jax.experimental.pallas import tpu as pltpu
from jax.sharding import PartitionSpec as P

F32 = jnp.float32
BF16 = jnp.bfloat16
MESH = pl.DeviceIdType.MESH
STEP = 16


def nt(left, right):
    return lax.dot_general(left, right, (((1,), (1,)), ((), ())), preferred_element_type=F32)


def nn(left, right):
    return lax.dot_general(left, right, (((1,), (0,)), ((), ())), preferred_element_type=F32)


def split2(x):
    high = x.astype(BF16)
    return high, (x - high.astype(F32)).astype(BF16)


def split3(x):
    high = x.astype(BF16).astype(F32)
    rest = x - high
    middle = rest.astype(BF16).astype(F32)
    return high, middle, rest - middle


def eliminate(m_ref, at):
    size = m_ref.shape[0]
    base = pl.multiple_of(at * STEP, STEP)
    rows = m_ref[pl.ds(base, STEP), :]
    turned = pltpu.roll(rows, size - at * STEP, 1)
    lane = lax.broadcasted_iota(jnp.int32, (STEP, size), 1)
    line = lax.broadcasted_iota(jnp.int32, (STEP, size), 0)
    line_narrow = lax.broadcasted_iota(jnp.int32, (STEP, 128), 0)
    columns = [jnp.broadcast_to(turned[:, j : j + 1], (STEP, 128)) for j in range(STEP)]
    inside = (lane >= base) & (lane < base + STEP)
    rows = jnp.where(inside, jnp.where(lane - base == line, 1.0, 0.0), rows)
    parts = [rows[:, p : p + 128] for p in range(0, size, 128)]
    for j in range(STEP):
        scale = lax.rsqrt(columns[j][j : j + 1, :])
        lower = jnp.where(line_narrow > j, columns[j] * scale, 0.0)
        for k in range(j + 1, STEP):
            columns[k] = columns[k] - lower * (columns[k][j : j + 1, :] * scale)
        for p in range(len(parts)):
            scaled = parts[p][j : j + 1, :] * scale
            parts[p] = jnp.where(line_narrow == j, scaled, parts[p] - lower * scaled)
    rows = jnp.concatenate(parts, 1)
    m_ref[pl.ds(base, STEP), :] = rows
    high, middle, low = split3(rows)
    left = jnp.concatenate([high, high, middle, high, middle, low], 0).astype(BF16)
    right = jnp.concatenate([high, middle, high, low, middle, high], 0).astype(BF16)
    change = lax.dot_general(left, right, (((0,), (0,)), ((), ())), preferred_element_type=F32)
    line_all = lax.broadcasted_iota(jnp.int32, (size, size), 0)
    lane_all = lax.broadcasted_iota(jnp.int32, (size, size), 1)
    whole = m_ref[...]
    inside = (lane_all >= base) & (lane_all < base + STEP)
    m_ref[...] = jnp.where(line_all >= base + STEP, jnp.where(inside, 0.0, whole) - change, whole)


def reduce_kernel(
    a_ref, t_ref, full_ref, inv_ref, c_ref,
    t_mem, t_high, t_low, g_part, g_recv, g_own, g_full, c_part, c_pair, c_recv, c_own,
    t_sem, ag_send, ag_recv, grs_send, grs_recv, gag_send, gag_recv,
    pair_send, pair_recv, crs_send, crs_recv, cag_send, cag_recv, last_send, last_recv,
):
    me = lax.axis_index("row")
    z = lax.axis_index("col")
    n_row = lax.axis_size("row")
    n_col = lax.axis_size("col")
    chip, core = me // 2, lax.rem(me, 2)
    n_chip = n_row // 2
    wide = a_ref.shape[0]
    n_b = full_ref.shape[0]
    n_t = t_ref.shape[0]
    half = c_part.shape[0] // 2
    block = half // n_chip
    own = n_b // n_row
    right, left = lax.rem(z + 1, n_col), lax.rem(z + n_col - 1, n_col)

    tile = half // 2
    loads = []
    for i in range(4):
        size = min(tile, n_t - i * tile)
        loads.append(pltpu.make_async_copy(t_ref.at[pl.ds(i * tile, size), :], t_mem.at[pl.ds(i * tile, size), :], t_sem.at[i]))
        loads[-1].start()

    barrier = pltpu.get_barrier_semaphore()
    for there in (left, right):
        pl.semaphore_signal(barrier, inc=1, device_id=(me, there), device_id_type=MESH)

    def greet(i, carry):
        pl.semaphore_signal(barrier, inc=1, device_id=(lax.rem(me + i, n_row), z), device_id_type=MESH)
        return carry

    lax.fori_loop(1, n_row, greet, 0)
    pl.semaphore_wait(barrier, n_row + 1)

    piece = 8
    n_piece = wide // piece

    def hop(way, step, q):
        owner = lax.rem(z - step + n_col, n_col) if way == 0 else lax.rem(z + step, n_col)
        place = pl.ds(pl.multiple_of(owner * wide + q * piece, piece), piece)
        source = a_ref.at[pl.ds(q * piece, piece), :] if step == 0 else full_ref.at[place, :]
        return pltpu.make_async_remote_copy(
            src_ref=source,
            dst_ref=full_ref.at[place, :],
            send_sem=ag_send.at[way, step, q],
            recv_sem=ag_recv.at[way, step, q],
            device_id=(me, right if way == 0 else left),
            device_id_type=MESH,
        )

    def taken(way, step):
        if step < n_col // 2 - 1:
            return range(n_piece)
        return range(n_piece // 2) if way == 0 else range(n_piece // 2, n_piece)

    hops = []
    for q in range(n_piece):
        for way in range(2):
            hops.append(hop(way, 0, q))
            hops[-1].start()
    full_ref[pl.ds(pl.multiple_of(z * wide, wide), wide), :] = a_ref[...]
    t_high[n_t:, :] = jnp.zeros((2 * half - n_t, t_high.shape[1]), BF16)
    t_low[n_t:, :] = jnp.zeros((2 * half - n_t, t_high.shape[1]), BF16)

    for step in range(n_col // 2):
        for q in range(n_piece):
            for way in range(2):
                if q in taken(way, step):
                    hop(way, step, q).wait_recv()
                    if step + 1 < n_col // 2 and q in taken(way, step + 1):
                        hops.append(hop(way, step + 1, q))
                        hops[-1].start()
        if step < 2:
            for i in (2 * step, 2 * step + 1):
                loads[i].wait()
                size = min(tile, n_t - i * tile)

                @pl.loop(0, size // 32)
                def _(k):
                    there = pl.ds(pl.multiple_of(i * tile + k * 32, 32), 32)
                    high, low = split2(t_mem[there, :])
                    t_high[there, :] = high
                    t_low[there, :] = low

    for copy in hops:
        copy.wait_send()

    full = full_ref[...]
    g_part[...] = lax.dot_general(full, full, (((1,), (1,)), ((), ())), precision=lax.Precision.HIGHEST, preferred_element_type=F32)

    def g_send(i, carry):
        there = lax.rem(me + i, n_row)
        pltpu.make_async_remote_copy(
            src_ref=g_part.at[pl.ds(pl.multiple_of(there * own, own), own), :],
            dst_ref=g_recv.at[me],
            send_sem=grs_send,
            recv_sem=grs_recv,
            device_id=(there, z),
            device_id_type=MESH,
        ).start()
        return carry

    lax.fori_loop(1, n_row, g_send, 0)
    g_recv[me] = g_part[pl.ds(pl.multiple_of(me * own, own), own), :]

    a_high, a_low = split2(full)

    def cross(start, size):
        for k in range(0, size, size // 4):
            there = pl.ds(pl.multiple_of(start + k, 16), size // 4)
            high, low = t_high[there, :], t_low[there, :]
            c_part[there, :] = nt(high, a_high) + (nt(high, a_low) + nt(low, a_high))

    cross((1 - core) * half, half)
    pair = pltpu.make_async_remote_copy(
        src_ref=c_part.at[pl.ds(pl.multiple_of((1 - core) * half, half), half), :],
        dst_ref=c_pair,
        send_sem=pair_send,
        recv_sem=pair_recv,
        device_id=(me + 1 - 2 * core, z),
        device_id_type=MESH,
    )
    pair.start()

    everyone = pl.ds(0, n_row - 1)
    pltpu.make_async_copy(g_recv.at[everyone], g_recv.at[everyone], grs_recv).wait()
    g_own[...] = jnp.sum(g_recv[...], axis=0)

    def g_spread(i, carry):
        pltpu.make_async_remote_copy(
            src_ref=g_own,
            dst_ref=g_full.at[pl.ds(pl.multiple_of(me * own, own), own), :],
            send_sem=gag_send,
            recv_sem=gag_recv,
            device_id=(lax.rem(me + i, n_row), z),
            device_id_type=MESH,
        ).start()
        return carry

    lax.fori_loop(1, n_row, g_spread, 0)
    g_full[pl.ds(pl.multiple_of(me * own, own), own), :] = g_own[...]

    cross(core * half, half)
    pair.wait()
    mine = pl.multiple_of(core * half, half)

    @pl.loop(0, n_chip)
    def _(k):
        there = pl.ds(pl.multiple_of(k * block, block), block)
        c_pair[there, :] = c_pair[there, :] + c_part[pl.ds(pl.multiple_of(mine + k * block, block), block), :]

    def c_send(i, carry):
        there = lax.rem(chip + i, n_chip)
        pltpu.make_async_remote_copy(
            src_ref=c_pair.at[pl.ds(pl.multiple_of(there * block, block), block), :],
            dst_ref=c_recv.at[chip],
            send_sem=crs_send,
            recv_sem=crs_recv,
            device_id=(there * 2 + core, z),
            device_id_type=MESH,
        ).start()
        return carry

    lax.fori_loop(1, n_chip, c_send, 0)
    c_recv[chip] = c_pair[pl.ds(pl.multiple_of(chip * block, block), block), :]

    rest = pl.ds(0, (n_row - 1) * own)
    pltpu.make_async_copy(g_full.at[rest, :], g_full.at[rest, :], gag_recv).wait()

    def some(at, carry):
        eliminate(g_full, at)
        return carry

    lax.fori_loop(0, 10, some, 0)

    others = pl.ds(0, n_chip - 1)
    pltpu.make_async_copy(c_recv.at[others], c_recv.at[others], crs_recv).wait()
    c_own[...] = jnp.sum(c_recv[...], axis=0)
    here = pl.ds(pl.multiple_of(mine + chip * block, block), block)

    def c_spread(i, carry):
        pltpu.make_async_remote_copy(
            src_ref=c_own,
            dst_ref=c_ref.at[here, :],
            send_sem=cag_send,
            recv_sem=cag_recv,
            device_id=(lax.rem(chip + i, n_chip) * 2 + core, z),
            device_id_type=MESH,
        ).start()
        return carry

    lax.fori_loop(1, n_chip, c_spread, 0)
    c_ref[here, :] = c_own[...]
    lax.fori_loop(10, n_b // STEP, some, 0)
    line = lax.broadcasted_iota(jnp.int32, (n_b, n_b), 0)
    lane = lax.broadcasted_iota(jnp.int32, (n_b, n_b), 1)
    inv_ref[...] = jnp.where(line >= lane, g_full[...], 0.0)

    fetched = pl.ds(0, (n_chip - 1) * block)
    pltpu.make_async_copy(c_ref.at[fetched, :], c_ref.at[fetched, :], cag_recv).wait()
    held = pl.ds(mine, half)
    last = pltpu.make_async_remote_copy(
        src_ref=c_ref.at[held, :],
        dst_ref=c_ref.at[held, :],
        send_sem=last_send,
        recv_sem=last_recv,
        device_id=(me + 1 - 2 * core, z),
        device_id_type=MESH,
    )
    last.start()
    pltpu.make_async_copy(g_recv.at[everyone], g_recv.at[everyone], grs_send).wait()
    pltpu.make_async_copy(g_full.at[rest, :], g_full.at[rest, :], gag_send).wait()
    pltpu.make_async_copy(c_recv.at[others], c_recv.at[others], crs_send).wait()
    pltpu.make_async_copy(c_ref.at[fetched, :], c_ref.at[fetched, :], cag_send).wait()
    last.wait()


def reduce_call(a, t, n_row, n_col):
    wide, rows = a.shape
    n_b = wide * n_col
    n_t = t.shape[0]
    unit = n_row * 16
    padded = -(-n_t // unit) * unit
    half, n_chip = padded // 2, n_row // 2
    block = half // n_chip
    own = n_b // n_row
    vmem = pl.BlockSpec(memory_space=pltpu.VMEM)
    dma = pltpu.SemaphoreType.DMA
    return pl.pallas_call(
        reduce_kernel,
        out_shape=(
            jax.ShapeDtypeStruct((n_b, rows), F32),
            jax.ShapeDtypeStruct((n_b, n_b), F32),
            jax.ShapeDtypeStruct((padded, n_b), F32),
        ),
        in_specs=[vmem, pl.BlockSpec(memory_space=pl.ANY)],
        out_specs=(vmem, vmem, vmem),
        scratch_shapes=[
            pltpu.VMEM((n_t, rows), F32),
            pltpu.VMEM((padded, rows), BF16),
            pltpu.VMEM((padded, rows), BF16),
            pltpu.VMEM((n_b, n_b), F32),
            pltpu.VMEM((n_row, own, n_b), F32),
            pltpu.VMEM((own, n_b), F32),
            pltpu.VMEM((n_b, n_b), F32),
            pltpu.VMEM((padded, n_b), F32),
            pltpu.VMEM((half, n_b), F32),
            pltpu.VMEM((n_chip, block, n_b), F32),
            pltpu.VMEM((block, n_b), F32),
            dma((4,)),
            dma((2, n_col // 2, wide // 8)),
            dma((2, n_col // 2, wide // 8)),
        ] + [dma] * 12,
        compiler_params=pltpu.CompilerParams(collective_id=0, has_side_effects=True, vmem_limit_bytes=48 * 2**20),
    )(a, t)


def update_kernel(full_ref, inv_ref, c_ref, t_ref, p_ref, r_ref, q_high, q_low):
    high, low = split2(inv_ref[...])

    @pl.when(pl.program_id(0) == 0)
    def _():
        a_high, a_low = split2(full_ref[...])
        q = nn(high, a_high) + (nn(high, a_low) + nn(low, a_high))
        q_high[...], q_low[...] = split2(q)

    c_high, c_low = split2(c_ref[...])
    p = nt(c_high, high) + (nt(c_high, low) + nt(c_low, high))
    p_ref[...] = p
    p_high, p_low = split2(p)
    r_ref[...] = t_ref[...] - (nn(p_high, q_high[...]) + (nn(p_high, q_low[...]) + nn(p_low, q_high[...])))


def update_call(full, inverse, c, t, tiles=4):
    n_b, rows = full.shape
    n_t = t.shape[0]
    tile = n_t // tiles
    return pl.pallas_call(
        update_kernel,
        grid=(tiles,),
        out_shape=(jax.ShapeDtypeStruct((n_t, n_b), F32), jax.ShapeDtypeStruct((n_t, rows), F32)),
        in_specs=[
            pl.BlockSpec((n_b, rows), lambda i: (0, 0)),
            pl.BlockSpec((n_b, n_b), lambda i: (0, 0)),
            pl.BlockSpec((tile, n_b), lambda i: (i, 0)),
            pl.BlockSpec((tile, rows), lambda i: (i, 0)),
        ],
        out_specs=(pl.BlockSpec((tile, n_b), lambda i: (i, 0)), pl.BlockSpec((tile, rows), lambda i: (i, 0))),
        scratch_shapes=[pltpu.VMEM((n_b, rows), BF16), pltpu.VMEM((n_b, rows), BF16)],
        compiler_params=pltpu.CompilerParams(vmem_limit_bytes=40 * 2**20),
    )(full, inverse, c, t)


def solution(mesh):
    n_row, n_col = mesh.shape["row"], mesh.shape["col"]

    def per_device(panel, trailing):
        a, t = panel.T, trailing.T
        full, inverse, c = reduce_call(a, t, n_row, n_col)
        projections, remainder = update_call(full, inverse, c, t)
        return projections, remainder.T

    return jax.shard_map(
        per_device,
        mesh=mesh,
        in_specs=(P("row", "col"), P("row", "col")),
        out_specs=(P("col", None), P("row", "col")),
        check_vma=False,
    )
```

time: 243 us -> 68.8 us (0.28)
  waiting for transfers between devices: 122 us -> 0 us
  Pallas kernels: 0 us -> 67 us
  other arithmetic: 56.1 us -> 0 us
  blocking collectives: 24.6 us -> 0 us
  matrix products: 18.8 us -> 0 us
  between operations: 15.5 us -> 0.66 us
  local copies, waits for them, and re-layouts: 5.15 us -> 1.04 us
    psum x1 -> x0, waiting for transfers between devices: 122 us -> none  [per_device(): cross_terms = lax.psum(cross_rows(trailing, panel_full), 'row')]
    pallas_call x0 -> x2, Pallas kernels: none -> 67 us  [the longest x1 60.5 us: reduce_call(): pl.pallas_call(reduce_kernel, out_shape=(jax.ShapeDtypeStruct((n_b, rows)...]
    another operation x9 -> x0, other arithmetic: 53.8 us -> none  [the longest x6 34.1 us: per_device(): lower_factor = jnp.linalg.cholesky(panel_gram)]
    all_gather x1 -> x0, blocking collectives: 24.6 us -> none  [per_device(): panel_full = lax.all_gather(panel, 'col', axis=1, tiled=True)]
    dot_general x3 -> x0, matrix products: 14.5 us -> none  [the longest x2 8.82 us: cross_rows(): lax.dot_general(left, right, (((0,), (0,)), ((), ())), precision=lax.Prec...]
    another operation x8 -> x0, matrix products: 4.29 us -> none  [the longest x6 3.82 us: solve_right(): jax.scipy.linalg.solve_triangular(lower_factor, terms.T, lower=True)]
    another operation x9 -> x0, local copies, waits for them, and re-layouts: 4.05 us -> none
  transfers between devices with their start and end apart: 1 -> 0, of which waited for: 1 -> 0; matrix products, arithmetic and copies ran while one was open for 0% -> 0% of each run, Pallas kernels for 0% -> 0%
where the time goes in v1:
time: 68.8 us; the launch traced here: 68.7 us
  Pallas kernels  67 us (97%)
  local copies, waits for them, and re-layouts  1.04 us (2%)
    pallas_call x1, Pallas kernels, reduce_call(): pl.pallas_call(reduce_kernel, out_shape=(jax.ShapeDtypeStruct((n_b, rows)...  60.5 us
    pallas_call x1, Pallas kernels, update_call(): pl.pallas_call(update_kernel, grid=(tiles,), out_shape=(jax.ShapeDtypeStr...  6.5 us

profile of v1, /device:TPU:1, one launch (start us, length us, event | category | flops | bytes accessed | tf_op | source)
XLA Modules:
  0.0 68.7 jit_solution(5550628798666927400)
XLA Ops:
  0.6 0.0 copy-start
  0.6 0.0 copy-start.1
  0.6 1.0 %copy-done.1 = f32[768,32]{0,1:T(8,128)S(1)} copy-done((f32[768,32]{0,1:T(8,128)S(1)}, f32[768,32]{0,1:T(8,128)}, u32[]{:S(2)}) %copy-start.1) | copy-done | bytes 98328
  1.7 60.5 %shard_map.41 = (f32[256,768]{1,0:T(8,128)S(1)}, f32[256,256]{1,0:T(8,128)S(1)}, f32[1536,256]{1,0:T(8,128)S(1)}) custom-call(f32[32,768]{1,0:T(8,128)S(1)} %bitcast.5, f32[1504,768]{1,0:T(8,128)} %bitcast.3), custom_call_target="tpu_custom_call" | custom-call | tf_op jit(solution)/shard_map/pallas_call | solution.py:299
  62.2 0.0 copy-done
  62.2 6.5 %shard_map.42 = (f32[1504,256]{1,0:T(8,128)}, f32[1504,768]{1,0:T(8,128)}) custom-call(f32[256,768]{1,0:T(8,128)S(1)} %get-tuple-element.7.full_ref, f32[256,256]{1,0:T(8,128)S(1)} %get-tuple-element.8.inv_ref, f32[1536,256]{1,0:T(8,128)S(1)} %get-tuple-element.9.c_ref, f32[1504,768]{1,0:T(8,128)S(1)} %bitcast.4), custom_call_target="tpu_custom_call" | custom-call | tf_op jit(solution)/shard_map/pallas_call | solution.py:348
Async XLA Ops:
  0.6 61.6 %copy-start = (f32[768,1504]{0,1:T(8,128)S(1)}, f32[768,1504]{0,1:T(8,128)}, u32[]{:S(2)}) copy-start(f32[768,1504]{0,1:T(8,128)} %param.3) | copy-start | bytes 13860868
  0.6 1.0 %copy-start.1 = (f32[768,32]{0,1:T(8,128)S(1)}, f32[768,32]{0,1:T(8,128)}, u32[]{:S(2)}) copy-start(f32[768,32]{0,1:T(8,128)} %param.2) | copy-start | bytes 294916

commit v2 on v1

v2 whole, which is shorter than its diff:
```python
import jax
import jax.numpy as jnp
from jax import lax
from jax.experimental import pallas as pl
from jax.experimental.pallas import tpu as pltpu
from jax.sharding import PartitionSpec as P

F32 = jnp.float32
BF16 = jnp.bfloat16
MESH = pl.DeviceIdType.MESH
STEP = 16
SIDE = 4
TILE = 256


def nt(left, right):
    return lax.dot_general(left, right, (((1,), (1,)), ((), ())), preferred_element_type=F32)


def nn(left, right):
    return lax.dot_general(left, right, (((1,), (0,)), ((), ())), preferred_element_type=F32)


def split2(x):
    high = x.astype(BF16)
    return high, (x - high.astype(F32)).astype(BF16)


def split3(x):
    high = x.astype(BF16).astype(F32)
    rest = x - high
    middle = rest.astype(BF16).astype(F32)
    return high, middle, rest - middle


def eliminate(m_ref, at):
    size = m_ref.shape[0]
    base = pl.multiple_of(at * STEP, STEP)
    rows = m_ref[pl.ds(base, STEP), :]
    turned = pltpu.roll(rows, size - at * STEP, 1)
    lane = lax.broadcasted_iota(jnp.int32, (STEP, size), 1)
    line = lax.broadcasted_iota(jnp.int32, (STEP, size), 0)
    line_narrow = lax.broadcasted_iota(jnp.int32, (STEP, 128), 0)
    columns = [jnp.broadcast_to(turned[:, j : j + 1], (STEP, 128)) for j in range(STEP)]
    inside = (lane >= base) & (lane < base + STEP)
    rows = jnp.where(inside, jnp.where(lane - base == line, 1.0, 0.0), rows)
    parts = [rows[:, p : p + 128] for p in range(0, size, 128)]
    for j in range(STEP):
        scale = lax.rsqrt(columns[j][j : j + 1, :])
        lower = jnp.where(line_narrow > j, columns[j] * scale, 0.0)
        for k in range(j + 1, STEP):
            columns[k] = columns[k] - lower * (columns[k][j : j + 1, :] * scale)
        for p in range(len(parts)):
            scaled = parts[p][j : j + 1, :] * scale
            parts[p] = jnp.where(line_narrow == j, scaled, parts[p] - lower * scaled)
    rows = jnp.concatenate(parts, 1)
    m_ref[pl.ds(base, STEP), :] = rows
    high, middle, low = split3(rows)
    left = jnp.concatenate([high, high, middle, high, middle, low], 0).astype(BF16)
    right = jnp.concatenate([high, middle, high, low, middle, high], 0).astype(BF16)
    change = lax.dot_general(left, right, (((0,), (0,)), ((), ())), preferred_element_type=F32)
    line_all = lax.broadcasted_iota(jnp.int32, (size, size), 0)
    lane_all = lax.broadcasted_iota(jnp.int32, (size, size), 1)
    whole = m_ref[...]
    inside = (lane_all >= base) & (lane_all < base + STEP)
    m_ref[...] = jnp.where(line_all >= base + STEP, jnp.where(inside, 0.0, whole) - change, whole)


def reduce_kernel(
    a_ref, t_ref, p_ref, qh_ref, ql_ref,
    full, t_mem, t_high, t_low, g_part, g_low, g_high, low_own, high_own, g_full, c_part, c_pair, c_recv, c_own, c_all, inv_high, inv_low,
    met, t_sem, a_sem, ag_send, ag_recv, low_send, low_recv, high_send, high_recv, lag_send, lag_recv, hag_send, hag_recv,
    pair_send, pair_recv, crs_send, crs_recv, cag_send, cag_recv, last_send, last_recv,
):
    me = lax.axis_index("row")
    z = lax.axis_index("col")
    n_row = lax.axis_size("row")
    n_col = lax.axis_size("col")
    chip, core = me // 2, lax.rem(me, 2)
    n_chip = n_row // 2
    y, x = chip // SIDE, lax.rem(chip, SIDE)
    wide = a_ref.shape[0]
    n_b = full.shape[0]
    n_t = t_ref.shape[0]
    half = c_part.shape[0] // 2
    block = half // n_chip
    low_rows = n_b // 2
    own = low_rows // n_chip
    right, left = lax.rem(z + 1, n_col), lax.rem(z + n_col - 1, n_col)
    partner = me + 1 - 2 * core

    def sit(row, column, on):
        return (row * SIDE + column) * 2 + on

    x_near = [sit(y, lax.rem(x + k, SIDE), core) for k in (1, SIDE - 1)]
    y_near = [sit(lax.rem(y + k, SIDE), x, core) for k in (1, SIDE - 1)]

    barrier = pltpu.get_barrier_semaphore()
    for there in (left, right):
        pl.semaphore_signal(barrier, inc=1, device_id=(me, there), device_id_type=MESH)
    for there in x_near + y_near + [partner]:
        pl.semaphore_signal(barrier, inc=1, device_id=(there, z), device_id_type=MESH)

    tile = half // 2
    loads = []
    for i in range(4):
        size = min(tile, n_t - i * tile)
        loads.append(pltpu.make_async_copy(t_ref.at[pl.ds(i * tile, size), :], t_mem.at[pl.ds(i * tile, size), :], t_sem.at[i]))
        loads[-1].start()
    own_panel = pltpu.make_async_copy(a_ref, full.at[pl.ds(pl.multiple_of(z * wide, wide), wide), :], a_sem)
    own_panel.start()
    pl.semaphore_wait(barrier, 7)

    def meet(stage):
        near = (x_near, y_near, y_near, [partner])[stage]
        for there in near:
            pl.semaphore_signal(met.at[stage], inc=1, device_id=(there, z), device_id_type=MESH)

    def met_all(stage):
        pl.semaphore_wait(met.at[stage], (2, 2, 2, 1)[stage])

    piece = 8
    n_piece = wide // piece

    def hop(way, step, q):
        owner = lax.rem(z - step + n_col, n_col) if way == 0 else lax.rem(z + step, n_col)
        place = pl.ds(pl.multiple_of(owner * wide + q * piece, piece), piece)
        source = a_ref.at[pl.ds(q * piece, piece), :] if step == 0 else full.at[place, :]
        return pltpu.make_async_remote_copy(
            src_ref=source,
            dst_ref=full.at[place, :],
            send_sem=ag_send.at[way, step, q],
            recv_sem=ag_recv.at[way, step, q],
            device_id=(me, right if way == 0 else left),
            device_id_type=MESH,
        )

    def taken(way, step):
        if step < n_col // 2 - 1:
            return range(n_piece)
        return range(n_piece // 2) if way == 0 else range(n_piece // 2, n_piece)

    hops = []
    for q in range(n_piece):
        for way in range(2):
            hops.append(hop(way, 0, q))
            hops[-1].start()
    meet(0)
    t_high[n_t:, :] = jnp.zeros((2 * half - n_t, t_high.shape[1]), BF16)
    t_low[n_t:, :] = jnp.zeros((2 * half - n_t, t_high.shape[1]), BF16)
    g_full[low_rows:, :low_rows] = jnp.zeros((n_b - low_rows, low_rows), F32)

    slot = 0
    slots = n_piece * (n_col // 2)
    share = 2 * half // slots
    for step in range(n_col // 2):
        for q in range(n_piece):
            first = slot * share
            if first % tile == 0:
                loads[first // tile].wait()
            count = min(share, n_t - first) // 32

            @pl.loop(0, count)
            def _(k):
                there = pl.ds(pl.multiple_of(first + k * 32, 32), 32)
                high, low = split2(t_mem[there, :])
                t_high[there, :] = high
                t_low[there, :] = low

            slot += 1
            for way in range(2):
                if q in taken(way, step):
                    hop(way, step, q).wait_recv()
                    if step + 1 < n_col // 2 and q in taken(way, step + 1):
                        hops.append(hop(way, step + 1, q))
                        hops[-1].start()
        met_all(step)
        if step < 3:
            meet(step + 1)

    own_panel.wait()
    a_full = full[...]
    g_part[...] = lax.dot_general(a_full, a_full, (((1,), (1,)), ((), ())), precision=lax.Precision.HIGHEST, preferred_element_type=F32)

    def low_at(k):
        return pl.ds(pl.multiple_of(k * own, own), own)

    def high_at(k):
        return pl.ds(pl.multiple_of(low_rows + k * own, own), own)

    upper = pl.ds(low_rows, n_b - low_rows)

    def low_copy(there):
        return pltpu.make_async_remote_copy(
            src_ref=g_part.at[low_at(there), :], dst_ref=g_low.at[me], send_sem=low_send, recv_sem=low_recv,
            device_id=(there * 2, z), device_id_type=MESH)

    def high_copy(there):
        return pltpu.make_async_remote_copy(
            src_ref=g_part.at[high_at(there), upper], dst_ref=g_high.at[me], send_sem=high_send, recv_sem=high_recv,
            device_id=(there * 2 + 1, z), device_id_type=MESH)

    def each_chip(start):
        def body(i, carry):
            start(lax.rem(chip + i, n_chip))
            return carry

        lax.fori_loop(1, n_chip, body, 0)

    each_chip(lambda there: low_copy(there).start())

    @pl.when(core == 1)
    def _():
        low_copy(chip).start()

    each_chip(lambda there: high_copy(there).start())

    @pl.when(core == 0)
    def _():
        high_copy(chip).start()
        g_low[me] = g_part[low_at(chip), :]

    @pl.when(core == 1)
    def _():
        g_high[me] = g_part[high_at(chip), low_rows:]

    a_high, a_low = split2(a_full)

    def cross(start, size):
        for k in range(0, size, size // 4):
            there = pl.ds(pl.multiple_of(start + k, 16), size // 4)
            high, low = t_high[there, :], t_low[there, :]
            c_part[there, :] = nt(high, a_high) + (nt(high, a_low) + nt(low, a_high))

    cross((1 - core) * half, half)
    pair = pltpu.make_async_remote_copy(
        src_ref=c_part.at[pl.ds(pl.multiple_of((1 - core) * half, half), half), :],
        dst_ref=c_pair,
        send_sem=pair_send,
        recv_sem=pair_recv,
        device_id=(partner, z),
        device_id_type=MESH,
    )
    pair.start()

    def await_all(ref, sem):
        pltpu.make_async_copy(ref, ref, sem).wait()

    def each_row(start):
        def body(i, carry):
            start(lax.rem(me + i, n_row))
            return carry

        lax.fori_loop(1, n_row, body, 0)

    @pl.when(core == 0)
    def _():
        await_all(g_low.at[pl.ds(0, n_row - 1)], low_recv)
        low_own[...] = jnp.sum(g_low[...], axis=0)
        each_row(lambda there: pltpu.make_async_remote_copy(
            src_ref=low_own, dst_ref=g_full.at[low_at(chip), :], send_sem=lag_send, recv_sem=lag_recv,
            device_id=(there, z), device_id_type=MESH).start())
        g_full[low_at(chip), :] = low_own[...]

    @pl.when(core == 1)
    def _():
        await_all(g_high.at[pl.ds(0, n_row - 1)], high_recv)
        high_own[...] = jnp.sum(g_high[...], axis=0)
        each_row(lambda there: pltpu.make_async_remote_copy(
            src_ref=high_own, dst_ref=g_full.at[high_at(chip), upper], send_sem=hag_send, recv_sem=hag_recv,
            device_id=(there, z), device_id_type=MESH).start())
        g_full[high_at(chip), low_rows:] = high_own[...]

    cross(core * half, half)
    pair.wait()
    mine = pl.multiple_of(core * half, half)

    @pl.loop(0, n_chip)
    def _(k):
        there = pl.ds(pl.multiple_of(k * block, block), block)
        c_pair[there, :] = c_pair[there, :] + c_part[pl.ds(pl.multiple_of(mine + k * block, block), block), :]

    each_chip(lambda there: pltpu.make_async_remote_copy(
        src_ref=c_pair.at[pl.ds(pl.multiple_of(there * block, block), block), :],
        dst_ref=c_recv.at[chip],
        send_sem=crs_send,
        recv_sem=crs_recv,
        device_id=(there * 2 + core, z),
        device_id_type=MESH,
    ).start())
    c_recv[chip] = c_pair[pl.ds(pl.multiple_of(chip * block, block), block), :]

    few = (n_chip - 1) * own

    @pl.when(core == 0)
    def _():
        await_all(g_full.at[pl.ds(0, few), :], lag_recv)
        await_all(g_full.at[pl.ds(low_rows, few + own), upper], hag_recv)

    @pl.when(core == 1)
    def _():
        await_all(g_full.at[pl.ds(0, few + own), :], lag_recv)
        await_all(g_full.at[pl.ds(low_rows, few), upper], hag_recv)

    def some(at, carry):
        eliminate(g_full, at)
        return carry

    lax.fori_loop(0, 10, some, 0)

    others = pl.ds(0, n_chip - 1)
    await_all(c_recv.at[others], crs_recv)
    c_own[...] = jnp.sum(c_recv[...], axis=0)
    here = pl.ds(pl.multiple_of(chip * block, block), block)
    each_chip(lambda there: pltpu.make_async_remote_copy(
        src_ref=c_own,
        dst_ref=c_all.at[here, :],
        send_sem=cag_send,
        recv_sem=cag_recv,
        device_id=(there * 2 + core, z),
        device_id_type=MESH,
    ).start())
    c_all[here, :] = c_own[...]
    lax.fori_loop(10, n_b // STEP, some, 0)

    line = lax.broadcasted_iota(jnp.int32, (n_b, n_b), 0)
    lane = lax.broadcasted_iota(jnp.int32, (n_b, n_b), 1)
    high, low = split2(jnp.where(line >= lane, g_full[...], 0.0))
    inv_high[...] = high
    inv_low[...] = low
    a_high, a_low = split2(full[...])
    q = nn(high, a_high) + (nn(high, a_low) + nn(low, a_high))
    qh_ref[...], ql_ref[...] = split2(q)

    fetched = pl.ds(0, (n_chip - 1) * block)
    await_all(c_all.at[fetched, :], cag_recv)
    quarter = half // 4
    lasts = []
    for k in range(4):
        there = pl.ds(k * quarter, quarter)
        c_high, c_low = split2(c_all[there, :])
        held = pl.ds(pl.multiple_of(mine + k * quarter, quarter), quarter)
        p_ref[held, :] = nt(c_high, inv_high[...]) + (nt(c_high, inv_low[...]) + nt(c_low, inv_high[...]))
        lasts.append(pltpu.make_async_remote_copy(
            src_ref=p_ref.at[held, :],
            dst_ref=p_ref.at[held, :],
            send_sem=last_send.at[k],
            recv_sem=last_recv.at[k],
            device_id=(partner, z),
            device_id_type=MESH,
        ))
        lasts[-1].start()

    for copy in hops:
        copy.wait_send()

    @pl.when(core == 0)
    def _():
        await_all(g_low.at[others], low_send)
        await_all(g_high.at[pl.ds(0, n_chip)], high_send)
        await_all(g_low.at[pl.ds(0, n_row - 1)], lag_send)

    @pl.when(core == 1)
    def _():
        await_all(g_low.at[pl.ds(0, n_chip)], low_send)
        await_all(g_high.at[others], high_send)
        await_all(g_high.at[pl.ds(0, n_row - 1)], hag_send)

    await_all(c_recv.at[others], crs_send)
    await_all(c_all.at[fetched, :], cag_send)
    for copy in lasts:
        copy.wait()


def reduce_call(a, t, n_row, n_col):
    wide, rows = a.shape
    n_b = wide * n_col
    n_t = t.shape[0]
    unit = n_row * 16
    padded = -(-n_t // unit) * unit
    half, n_chip = padded // 2, n_row // 2
    block = half // n_chip
    own = n_b // n_row
    vmem = pl.BlockSpec(memory_space=pltpu.VMEM)
    dma = pltpu.SemaphoreType.DMA
    return pl.pallas_call(
        reduce_kernel,
        out_shape=(
            jax.ShapeDtypeStruct((padded, n_b), F32),
            jax.ShapeDtypeStruct((n_b, rows), BF16),
            jax.ShapeDtypeStruct((n_b, rows), BF16),
        ),
        in_specs=[pl.BlockSpec(memory_space=pl.ANY), pl.BlockSpec(memory_space=pl.ANY)],
        out_specs=(vmem, vmem, vmem),
        scratch_shapes=[
            pltpu.VMEM((n_b, rows), F32),
            pltpu.VMEM((n_t, rows), F32),
            pltpu.VMEM((padded, rows), BF16),
            pltpu.VMEM((padded, rows), BF16),
            pltpu.VMEM((n_b, n_b), F32),
            pltpu.VMEM((n_row, own, n_b), F32),
            pltpu.VMEM((n_row, own, n_b // 2), F32),
            pltpu.VMEM((own, n_b), F32),
            pltpu.VMEM((own, n_b // 2), F32),
            pltpu.VMEM((n_b, n_b), F32),
            pltpu.VMEM((padded, n_b), F32),
            pltpu.VMEM((half, n_b), F32),
            pltpu.VMEM((n_chip, block, n_b), F32),
            pltpu.VMEM((block, n_b), F32),
            pltpu.VMEM((half, n_b), F32),
            pltpu.VMEM((n_b, n_b), BF16),
            pltpu.VMEM((n_b, n_b), BF16),
            pltpu.SemaphoreType.REGULAR((4,)),
            dma((4,)),
            dma,
            dma((2, n_col // 2, wide // 8)),
            dma((2, n_col // 2, wide // 8)),
        ] + [dma] * 14 + [dma((4,))] * 2,
        compiler_params=pltpu.CompilerParams(collective_id=0, has_side_effects=True, vmem_limit_bytes=48 * 2**20),
    )(a, t)


def update_kernel(p_ref, qh_ref, ql_ref, t_ref, p_out, r_out, r_mem, p_sem, r_sem):
    n_t = t_ref.shape[0]
    first = pltpu.make_async_copy(p_ref.at[pl.ds(0, n_t), :], p_out, p_sem)
    first.start()
    q_high, q_low = qh_ref[...], ql_ref[...]
    copies = []
    for i, start in enumerate(range(0, n_t, TILE)):
        there = pl.ds(start, min(TILE, n_t - start))
        p_high, p_low = split2(p_ref[there, :])
        r_mem[there, :] = t_ref[there, :] - (nn(p_high, q_high) + (nn(p_high, q_low) + nn(p_low, q_high)))
        copies.append(pltpu.make_async_copy(r_mem.at[there, :], r_out.at[there, :], r_sem.at[i]))
        copies[-1].start()
    first.wait()
    for copy in copies:
        copy.wait()


def update_call(p, q_high, q_low, t):
    n_b, rows = q_high.shape
    n_t = t.shape[0]
    vmem = pl.BlockSpec(memory_space=pltpu.VMEM)
    hbm = pl.BlockSpec(memory_space=pltpu.HBM)
    return pl.pallas_call(
        update_kernel,
        out_shape=(jax.ShapeDtypeStruct((n_t, n_b), F32), jax.ShapeDtypeStruct((n_t, rows), F32)),
        in_specs=[vmem] * 4,
        out_specs=(hbm, hbm),
        scratch_shapes=[
            pltpu.VMEM((n_t, rows), F32),
            pltpu.SemaphoreType.DMA,
            pltpu.SemaphoreType.DMA((-(-n_t // TILE),)),
        ],
        compiler_params=pltpu.CompilerParams(vmem_limit_bytes=24 * 2**20),
    )(p, q_high, q_low, t)


def solution(mesh):
    n_row, n_col = mesh.shape["row"], mesh.shape["col"]

    def per_device(panel, trailing):
        a, t = pltpu.with_memory_space_constraint(panel.T, pltpu.HBM), trailing.T
        p, q_high, q_low = reduce_call(a, t, n_row, n_col)
        projections, remainder = update_call(p, q_high, q_low, t)
        return projections, remainder.T

    return jax.shard_map(
        per_device,
        mesh=mesh,
        in_specs=(P("row", "col"), P("row", "col")),
        out_specs=(P("col", None), P("row", "col")),
        check_vma=False,
    )
```

time: 68.8 us -> 63.5 us (0.923)
  Pallas kernels: 67 us -> 62.7 us
  local copies, waits for them, and re-layouts: 1.04 us -> 0.01 us
    pallas_call x2, Pallas kernels: 67 us -> 62.7 us  [the longest x1 59.3 us: reduce_call(): pl.pallas_call(reduce_kernel, out_shape=(jax.ShapeDtypeStruct((padded, n_...]
    unnamed x4 -> x2, local copies, waits for them, and re-layouts: 1.04 us -> 0.01 us
where the time goes in v2:
time: 63.5 us; the launch traced here: 63.4 us
  Pallas kernels  62.7 us (99%)
  between operations  0.65 us (1%)
    pallas_call x1, Pallas kernels, reduce_call(): pl.pallas_call(reduce_kernel, out_shape=(jax.ShapeDtypeStruct((padded, n_...  59.3 us
    pallas_call x1, Pallas kernels, update_call(): pl.pallas_call(update_kernel, out_shape=(jax.ShapeDtypeStruct((n_t, n_b),...  3.41 us

profile of v2, /device:TPU:1, one launch (start us, length us, event | category | flops | bytes accessed | tf_op | source)
XLA Modules:
  0.0 63.4 jit_solution(2480552254825704343)
XLA Ops:
  0.6 0.0 copy-start
  0.6 59.3 %shard_map.41 = (f32[1536,256]{1,0:T(8,128)S(1)}, bf16[256,768]{1,0:T(8,128)(2,1)S(1)}, bf16[256,768]{1,0:T(8,128)(2,1)S(1)}) custom-call(f32[32,768]{1,0:T(8,128)} %bitcast.5, f32[1504,768]{1,0:T(8,128)} %bitcast.3), custom_call_target="tpu_custom_call" | custom-call | tf_op jit(solution)/shard_map/pallas_call | solution.py:386
  60.0 0.0 copy-done
  60.0 3.4 %shard_map.42 = (f32[1504,256]{1,0:T(8,128)}, f32[1504,768]{1,0:T(8,128)}) custom-call(f32[1536,256]{1,0:T(8,128)S(1)} %get-tuple-element.7.p_ref, bf16[256,768]{1,0:T(8,128)(2,1)S(1)} %get-tuple-element.8.qh_ref, bf16[256,768]{1,0:T(8,128)(2,1)S(1)} %get-tuple-element.9.ql_ref, f32[1504,768]{1,0:T(8,128)S(1)} %bitcast.4), custom_call_target="tpu_custom_call" | custom-call | tf_op jit(solution)/shard_map/pallas_call | solution.py:445
Async XLA Ops:
  0.6 59.3 %copy-start = (f32[768,1504]{0,1:T(8,128)S(1)}, f32[768,1504]{0,1:T(8,128)}, u32[]{:S(2)}) copy-start(f32[768,1504]{0,1:T(8,128)} %param.3) | copy-start | bytes 13860868
